TPU v7x, 256 devices: a whole 4x4x8 slice. The times are simulated.
256 devices in a mesh: ctx: 64 (over z, y_lo, x), kvh: 4 (over y_hi, core).
Axes of the slice: x: 4, y: 4 (y_hi: 2, y_lo: 2; y = y_hi * 2 + y_lo), z: 8, core: 2. Of those that a mesh axis runs over, the one named last changes fastest.
Arguments:
- queries: bfloat16 [16384, 64, 128], P('ctx', 'kvh'), may hold values from -6 to 6
- keys: bfloat16 [16384, 8, 128], P(('ctx', 'kvh')), may hold values from -6 to 6
- values: bfloat16 [16384, 8, 128], P(('ctx', 'kvh')), may hold values from -6 to 6
- doc_blocks: int32 [32], replicated, may hold values from 1 to 14, 128 in all
Outputs:
- attended: bfloat16 [16384, 64, 128], P('ctx', 'kvh')
Inputs may be any that keep to these rules, and one draw needn't show every extreme that they name: document i covers doc_blocks[i] * 128 tokens; the lengths sum to 16384 tokens.
All inputs are finite; a program needn't handle non-finite values.
Results may differ from a plain program's by a relative error of at most 0.004.
Values may be sent and summed in bfloat16 or wider, within the bound.
A program may use at most 64 MiB of HBM per device.

v0:
```python
import math

import jax
import jax.numpy as jnp
from jax import lax
from jax.sharding import PartitionSpec as P

BLOCK = 128


negative = -1e30


def passed_along(shard, axis, by):
    size = lax.axis_size(axis)
    pairs = [(i, i + by) for i in range(size) if 0 <= i + by < size]
    return lax.ppermute(shard, axis, pairs)


def segment_of(positions, doc_ends):
    return jnp.sum((doc_ends[None, :] <= positions[:, None]).astype(jnp.int32), axis=1)


def body(queries, keys, values, doc_blocks):
    key_rows, value_rows = (
        lax.all_to_all(keys, "kvh", split_axis=1, concat_axis=0, tiled=True),
        lax.all_to_all(values, "kvh", split_axis=1, concat_axis=0, tiled=True),
    )
    rows = key_rows.shape[0]
    kv_count = key_rows.shape[1]
    query_heads = queries.shape[1]
    group = query_heads // kv_count
    depth = queries.shape[2]
    scale = 1.0 / math.sqrt(depth)
    sections = min(3, lax.axis_size("ctx") // 4)
    behind = 2**sections - 1
    own_index = lax.axis_index("ctx")
    doc_ends = jnp.cumsum(doc_blocks, dtype=jnp.int32) * BLOCK
    query_pos = own_index * rows + jnp.arange(rows, dtype=jnp.int32)
    query_seg = segment_of(query_pos, doc_ends)
    grouped = queries.reshape(rows, kv_count, group, depth)
    stacked = jnp.stack([key_rows, value_rows])
    start_state = (
        jnp.full((kv_count, group, rows), negative, jnp.float32),
        jnp.zeros((kv_count, group, rows), jnp.float32),
        jnp.zeros((kv_count, group, rows, depth), jnp.float32),
    )

    def update(state, block, key_start):
        key_pos = key_start + jnp.arange(block.shape[1], dtype=jnp.int32)
        key_seg = segment_of(key_pos, doc_ends)
        allowed = (
            (key_seg[None, :] == query_seg[:, None])
            & (key_pos[None, :] <= query_pos[:, None])
            & (key_pos[None, :] >= 0)
        )
        top_old, total_old, summed_old = state
        scores = (
            jnp.einsum("tkgd,skd->kgts", grouped, block[0], preferred_element_type=jnp.float32)
            * scale
        )
        scores = jnp.where(allowed[None, None], scores, negative)
        top_new = jnp.maximum(top_old, jnp.max(scores, axis=-1))
        fading = jnp.exp(top_old - top_new)
        weights = jnp.where(allowed[None, None], jnp.exp(scores - top_new[..., None]), 0.0)
        total_new = total_old * fading + jnp.sum(weights, axis=-1)
        product = jnp.einsum(
            "kgts,skd->kgtd",
            weights.astype(jnp.bfloat16),
            block[1],
            preferred_element_type=jnp.float32,
        )
        summed_new = summed_old * fading[..., None] + product
        return (top_new, total_new, summed_new)

    state = update(start_state, stacked, own_index * rows)
    moving = stacked
    for distance in range(1, behind + 1):
        moving = passed_along(moving, "ctx", 1)
        state = update(state, moving, (own_index - distance) * rows)
    top_final, total_final, summed_final = state
    output = (
        (summed_final / total_final[..., None])
        .transpose(2, 0, 1, 3)
        .reshape(rows, query_heads, depth)
    )
    return output.astype(jnp.bfloat16)


def solution(mesh):
    in_specs = (
        P("ctx", "kvh", None),
        P(("ctx", "kvh"), None, None),
        P(("ctx", "kvh"), None, None),
        P(),
    )
    out_specs = P("ctx", "kvh", None)
    return jax.shard_map(body, mesh=mesh, in_specs=in_specs, out_specs=out_specs, check_vma=False)
```

profile of v0, /device:TPU:128, one launch (start us, length us, event | category | flops | bytes accessed | tf_op | source)
XLA Modules:
  0.0 137.9 jit_solution(4489591274829074443)
XLA Ops:
  0.0 1.6 %copy.68 = bf16[64,8,128]{2,0,1:T(8,128)(2,1)} copy(bf16[64,8,128]{2,1,0:T(8,128)(2,1)} %param.5) | data formatting | bytes 262144 | tf_op args[1]
  1.7 4.5 %all-to-all-start = ((bf16[64,8,128]{2,0,1:T(8,128)(2,1)}), bf16[64,8,128]{2,0,1:T(8,128)(2,1)S(1)}, u32[]{:S(2)}, u32[]{:S(2)}) async-start(bf16[64,8,128]{2,0,1:T(8,128)(2,1)} %copy.68), calls=%async_computation | async-start | bytes 262144 | tf_op jit(solution)/shard_map/all_to_all | solution.py:26
  7.1 1.6 %copy.71 = bf16[64,8,128]{2,0,1:T(8,128)(2,1)} copy(bf16[64,8,128]{2,1,0:T(8,128)(2,1)} %param.6) | data formatting | bytes 262144 | tf_op args[2]
  9.7 2.5 %all-to-all-done = bf16[64,8,128]{2,0,1:T(8,128)(2,1)S(1)} async-done(((bf16[64,8,128]{2,0,1:T(8,128)(2,1)}), bf16[64,8,128]{2,0,1:T(8,128)(2,1)S(1)}, u32[]{:S(2)}, u32[]{:S(2)}) %all-to-all-start) | async-done | bytes 131104 | tf_op jit(solution)/shard_map/all_to_all | solution.py:26
  12.3 3.3 %all-to-all-start.1 = ((bf16[64,8,128]{2,0,1:T(8,128)(2,1)}), bf16[64,8,128]{2,0,1:T(8,128)(2,1)S(1)}, u32[]{:S(2)}, u32[]{:S(2)}) async-start(bf16[64,8,128]{2,0,1:T(8,128)(2,1)} %copy.71), calls=%async_computation.1 | async-start | bytes 262144 | tf_op jit(solution)/shard_map/all_to_all | solution.py:27
  15.9 5.8 %all-to-all-done.1 = bf16[64,8,128]{2,0,1:T(8,128)(2,1)S(1)} async-done(((bf16[64,8,128]{2,0,1:T(8,128)(2,1)}), bf16[64,8,128]{2,0,1:T(8,128)(2,1)S(1)}, u32[]{:S(2)}, u32[]{:S(2)}) %all-to-all-start.1) | async-done | bytes 131104 | tf_op jit(solution)/shard_map/all_to_all | solution.py:27
  21.7 3.4 %collective-permute-start = (bf16[2,256,2,128]{3,1,2,0:T(8,128)(2,1)S(1)}, bf16[2,256,2,128]{3,1,2,0:T(8,128)(2,1)S(1)}, u32[]{:S(2)}, u32[]{:S(2)}) collective-permute-start(bf16[2,256,2,128]{3,1,2,0:T(8,128)(2,1)S(1)} %pad_maximum_fusion), channel_id=1, source_target_pairs={{0,4},{4,8},{8,12},{12,16},{16,20},{20,24},{24,28},{28,32},{32,36}... | collective-permute-start | bytes 786440 | tf_op jit(solution)/shard_map/ppermute | solution.py:17
  26.1 9.5 %collective-permute-done = bf16[2,256,2,128]{3,1,2,0:T(8,128)(2,1)S(1)} collective-permute-done((bf16[2,256,2,128]{3,1,2,0:T(8,128)(2,1)S(1)}, bf16[2,256,2,128]{3,1,2,0:T(8,128)(2,1)S(1)}, u32[]{:S(2)}, u32[]{:S(2)}) %collective-permute-start) | collective-permute-done | bytes 262176 | tf_op jit(solution)/shard_map/ppermute | solution.py:17
  35.5 1.9 %collective-permute-start.1 = (bf16[2,256,2,128]{3,1,2,0:T(8,128)(2,1)S(1)}, bf16[2,256,2,128]{3,1,2,0:T(8,128)(2,1)S(1)}, u32[]{:S(2)}, u32[]{:S(2)}) collective-permute-start(bf16[2,256,2,128]{3,1,2,0:T(8,128)(2,1)S(1)} %collective-permute-done), channel_id=1, source_target_pairs={{0,4},{4,8},{8,12},{12,16},{16,20},{20,24},{24,28},{28,32},{32,36}... | collective-permute-start | bytes 786440 | tf_op jit(solution)/shard_map/ppermute | solution.py:17
  38.4 10.0 %collective-permute-done.1 = bf16[2,256,2,128]{3,1,2,0:T(8,128)(2,1)S(1)} collective-permute-done((bf16[2,256,2,128]{3,1,2,0:T(8,128)(2,1)S(1)}, bf16[2,256,2,128]{3,1,2,0:T(8,128)(2,1)S(1)}, u32[]{:S(2)}, u32[]{:S(2)}) %collective-permute-start.1) | collective-permute-done | bytes 262176 | tf_op jit(solution)/shard_map/ppermute | solution.py:17
  48.4 1.9 %collective-permute-start.2 = (bf16[2,256,2,128]{3,1,2,0:T(8,128)(2,1)S(1)}, bf16[2,256,2,128]{3,1,2,0:T(8,128)(2,1)S(1)}, u32[]{:S(2)}, u32[]{:S(2)}) collective-permute-start(bf16[2,256,2,128]{3,1,2,0:T(8,128)(2,1)S(1)} %collective-permute-done.1), channel_id=1, source_target_pairs={{0,4},{4,8},{8,12},{12,16},{16,20},{20,24},{24,28},{28,32},{32,36}... | collective-permute-start | bytes 786440 | tf_op jit(solution)/shard_map/ppermute | solution.py:17
  51.2 9.6 %collective-permute-done.2 = bf16[2,256,2,128]{3,1,2,0:T(8,128)(2,1)S(1)} collective-permute-done((bf16[2,256,2,128]{3,1,2,0:T(8,128)(2,1)S(1)}, bf16[2,256,2,128]{3,1,2,0:T(8,128)(2,1)S(1)}, u32[]{:S(2)}, u32[]{:S(2)}) %collective-permute-start.2) | collective-permute-done | bytes 262176 | tf_op jit(solution)/shard_map/ppermute | solution.py:17
  60.9 1.9 %collective-permute-start.3 = (bf16[2,256,2,128]{3,1,2,0:T(8,128)(2,1)S(1)}, bf16[2,256,2,128]{3,1,2,0:T(8,128)(2,1)S(1)}, u32[]{:S(2)}, u32[]{:S(2)}) collective-permute-start(bf16[2,256,2,128]{3,1,2,0:T(8,128)(2,1)S(1)} %collective-permute-done.2), channel_id=1, source_target_pairs={{0,4},{4,8},{8,12},{12,16},{16,20},{20,24},{24,28},{28,32},{32,36}... | collective-permute-start | bytes 786440 | tf_op jit(solution)/shard_map/ppermute | solution.py:17
  63.7 9.6 %collective-permute-done.3 = bf16[2,256,2,128]{3,1,2,0:T(8,128)(2,1)S(1)} collective-permute-done((bf16[2,256,2,128]{3,1,2,0:T(8,128)(2,1)S(1)}, bf16[2,256,2,128]{3,1,2,0:T(8,128)(2,1)S(1)}, u32[]{:S(2)}, u32[]{:S(2)}) %collective-permute-start.3) | collective-permute-done | bytes 262176 | tf_op jit(solution)/shard_map/ppermute | solution.py:17
  73.3 1.9 %collective-permute-start.4 = (bf16[2,256,2,128]{3,1,2,0:T(8,128)(2,1)S(1)}, bf16[2,256,2,128]{3,1,2,0:T(8,128)(2,1)S(1)}, u32[]{:S(2)}, u32[]{:S(2)}) collective-permute-start(bf16[2,256,2,128]{3,1,2,0:T(8,128)(2,1)S(1)} %collective-permute-done.3), channel_id=1, source_target_pairs={{0,4},{4,8},{8,12},{12,16},{16,20},{20,24},{24,28},{28,32},{32,36}... | collective-permute-start | bytes 786440 | tf_op jit(solution)/shard_map/ppermute | solution.py:17
  76.2 9.6 %collective-permute-done.4 = bf16[2,256,2,128]{3,1,2,0:T(8,128)(2,1)S(1)} collective-permute-done((bf16[2,256,2,128]{3,1,2,0:T(8,128)(2,1)S(1)}, bf16[2,256,2,128]{3,1,2,0:T(8,128)(2,1)S(1)}, u32[]{:S(2)}, u32[]{:S(2)}) %collective-permute-start.4) | collective-permute-done | bytes 262176 | tf_op jit(solution)/shard_map/ppermute | solution.py:17
  85.8 1.9 %collective-permute-start.5 = (bf16[2,256,2,128]{3,1,2,0:T(8,128)(2,1)S(1)}, bf16[2,256,2,128]{3,1,2,0:T(8,128)(2,1)S(1)}, u32[]{:S(2)}, u32[]{:S(2)}) collective-permute-start(bf16[2,256,2,128]{3,1,2,0:T(8,128)(2,1)S(1)} %collective-permute-done.4), channel_id=1, source_target_pairs={{0,4},{4,8},{8,12},{12,16},{16,20},{20,24},{24,28},{28,32},{32,36}... | collective-permute-start | bytes 786440 | tf_op jit(solution)/shard_map/ppermute | solution.py:17
  88.6 9.6 %collective-permute-done.5 = bf16[2,256,2,128]{3,1,2,0:T(8,128)(2,1)S(1)} collective-permute-done((bf16[2,256,2,128]{3,1,2,0:T(8,128)(2,1)S(1)}, bf16[2,256,2,128]{3,1,2,0:T(8,128)(2,1)S(1)}, u32[]{:S(2)}, u32[]{:S(2)}) %collective-permute-start.5) | collective-permute-done | bytes 262176 | tf_op jit(solution)/shard_map/ppermute | solution.py:17
  98.3 2.1 %collective-permute-start.6 = (bf16[2,256,2,128]{3,1,2,0:T(8,128)(2,1)S(1)}, bf16[2,256,2,128]{3,1,2,0:T(8,128)(2,1)S(1)}, u32[]{:S(2)}, u32[]{:S(2)}) collective-permute-start(bf16[2,256,2,128]{3,1,2,0:T(8,128)(2,1)S(1)} %collective-permute-done.5), channel_id=1, source_target_pairs={{0,4},{4,8},{8,12},{12,16},{16,20},{20,24},{24,28},{28,32},{32,36}... | collective-permute-start | bytes 786440 | tf_op jit(solution)/shard_map/ppermute | solution.py:17
  101.3 9.5 %collective-permute-done.6 = bf16[2,256,2,128]{3,1,2,0:T(8,128)(2,1)S(1)} collective-permute-done((bf16[2,256,2,128]{3,1,2,0:T(8,128)(2,1)S(1)}, bf16[2,256,2,128]{3,1,2,0:T(8,128)(2,1)S(1)}, u32[]{:S(2)}, u32[]{:S(2)}) %collective-permute-start.6) | collective-permute-done | bytes 262176 | tf_op jit(solution)/shard_map/ppermute | solution.py:17
  121.3 1.6 %fusion.34 = f32[2,8,256,128]{3,2,1,0:T(8,128)S(1)} fusion(f32[2,256,256,8]{2,1,3,0:T(8,128)S(1)} %get-tuple-element.51, f32[2,8,256]{2,1,0:T(8,128)S(1)} %get-tuple-element.27, pred[256,256]{0,1:T(8,128)(4,1)S(1)} %get-tuple-element.39, bf16[2,256,2,128]{3,1,2,0:T(8,128)(2,1)S(1)} %collective-permute-done.1), kind=kOutput, calls=%fused_computation.45 | convolution fusion | flops 273678336 | bytes 6504448 | tf_op jit(solution)/shard_map/kgts,skd->kgtd/dot_general | solution.py:67
  123.0 1.4 %fusion.36 = f32[2,8,256,128]{3,2,1,0:T(8,128)S(1)} fusion(f32[2,256,256,8]{2,1,3,0:T(8,128)S(1)} %get-tuple-element.53, f32[2,8,256]{2,1,0:T(8,128)S(1)} %get-tuple-element.28, pred[256,256]{0,1:T(8,128)(4,1)S(1)} %get-tuple-element.38, bf16[2,256,2,128]{3,1,2,0:T(8,128)(2,1)S(1)} %collective-permute-done), kind=kOutput, calls=%fused_computation.46 | convolution fusion | flops 273678336 | bytes 6504448 | tf_op jit(solution)/shard_map/kgts,skd->kgtd/dot_general | solution.py:67
  129.9 6.4 %fusion.41 = bf16[256,2,8,128]{3,0,2,1:T(8,128)(2,1)S(1)} fusion(f32[2,8,256,128]{3,2,1,0:T(8,128)S(1)} %fusion.26, f32[2,8,256,128]{3,2,1,0:T(8,128)S(1)} %fusion.28, f32[2,8,256,128]{3,2,1,0:T(8,128)S(1)} %fusion.30, f32[2,8,256,128]{3,2,1,0:T(8,128)S(1)} %fusion.32, f32[2,8,256,128]{3,2,1,0:T(8,128)S(1)} %fusion.34, f32[2,8,256,128]{3,2,1,0:T(8,128)S(1)} %fusion.36, ...), kind=kOutput, calls=%fused_computation.50 | convolution fusion | flops 282591232 | bytes 20283392 | tf_op jit(solution)/shard_map/kgts,skd->kgtd/dot_general | solution.py:67
  136.3 1.6 %copy.88 = bf16[256,16,128]{2,1,0:T(8,128)(2,1)} copy(bf16[256,16,128]{2,0,1:T(8,128)(2,1)S(1)} %bitcast.386) | data formatting | bytes 2097152 | tf_op jit(solution)/shard_map/convert_element_type | solution.py:87
  (43 shorter events, 24.7 us)
Async XLA Ops:
  0.0 25.1 %copy-start = (bf16[256,16,128]{2,1,0:T(8,128)(2,1)S(1)}, bf16[256,16,128]{2,1,0:T(8,128)(2,1)}, u32[]{:S(2)}) copy-start(bf16[256,16,128]{2,1,0:T(8,128)(2,1)} %param.4) | copy-start | bytes 3145732
  1.7 10.6 %all-to-all-start = ((bf16[64,8,128]{2,0,1:T(8,128)(2,1)}), bf16[64,8,128]{2,0,1:T(8,128)(2,1)S(1)}, u32[]{:S(2)}, u32[]{:S(2)}) async-start(bf16[64,8,128]{2,0,1:T(8,128)(2,1)} %copy.68), calls=%async_computation | async-start | bytes 262144 | tf_op jit(solution)/shard_map/all_to_all | solution.py:26
  12.3 9.4 %all-to-all-start.1 = ((bf16[64,8,128]{2,0,1:T(8,128)(2,1)}), bf16[64,8,128]{2,0,1:T(8,128)(2,1)S(1)}, u32[]{:S(2)}, u32[]{:S(2)}) async-start(bf16[64,8,128]{2,0,1:T(8,128)(2,1)} %copy.71), calls=%async_computation.1 | async-start | bytes 262144 | tf_op jit(solution)/shard_map/all_to_all | solution.py:27
  21.7 13.8 %collective-permute-start = (bf16[2,256,2,128]{3,1,2,0:T(8,128)(2,1)S(1)}, bf16[2,256,2,128]{3,1,2,0:T(8,128)(2,1)S(1)}, u32[]{:S(2)}, u32[]{:S(2)}) collective-permute-start(bf16[2,256,2,128]{3,1,2,0:T(8,128)(2,1)S(1)} %pad_maximum_fusion), channel_id=1, source_target_pairs={{0,4},{4,8},{8,12},{12,16},{16,20},{20,24},{24,28},{28,32},{32,36}... | collective-permute-start | bytes 786440 | tf_op jit(solution)/shard_map/ppermute | solution.py:17
  35.5 12.9 %collective-permute-start.1 = (bf16[2,256,2,128]{3,1,2,0:T(8,128)(2,1)S(1)}, bf16[2,256,2,128]{3,1,2,0:T(8,128)(2,1)S(1)}, u32[]{:S(2)}, u32[]{:S(2)}) collective-permute-start(bf16[2,256,2,128]{3,1,2,0:T(8,128)(2,1)S(1)} %collective-permute-done), channel_id=1, source_target_pairs={{0,4},{4,8},{8,12},{12,16},{16,20},{20,24},{24,28},{28,32},{32,36}... | collective-permute-start | bytes 786440 | tf_op jit(solution)/shard_map/ppermute | solution.py:17
  48.4 12.5 %collective-permute-start.2 = (bf16[2,256,2,128]{3,1,2,0:T(8,128)(2,1)S(1)}, bf16[2,256,2,128]{3,1,2,0:T(8,128)(2,1)S(1)}, u32[]{:S(2)}, u32[]{:S(2)}) collective-permute-start(bf16[2,256,2,128]{3,1,2,0:T(8,128)(2,1)S(1)} %collective-permute-done.1), channel_id=1, source_target_pairs={{0,4},{4,8},{8,12},{12,16},{16,20},{20,24},{24,28},{28,32},{32,36}... | collective-permute-start | bytes 786440 | tf_op jit(solution)/shard_map/ppermute | solution.py:17
  60.9 12.5 %collective-permute-start.3 = (bf16[2,256,2,128]{3,1,2,0:T(8,128)(2,1)S(1)}, bf16[2,256,2,128]{3,1,2,0:T(8,128)(2,1)S(1)}, u32[]{:S(2)}, u32[]{:S(2)}) collective-permute-start(bf16[2,256,2,128]{3,1,2,0:T(8,128)(2,1)S(1)} %collective-permute-done.2), channel_id=1, source_target_pairs={{0,4},{4,8},{8,12},{12,16},{16,20},{20,24},{24,28},{28,32},{32,36}... | collective-permute-start | bytes 786440 | tf_op jit(solution)/shard_map/ppermute | solution.py:17
  73.3 12.5 %collective-permute-start.4 = (bf16[2,256,2,128]{3,1,2,0:T(8,128)(2,1)S(1)}, bf16[2,256,2,128]{3,1,2,0:T(8,128)(2,1)S(1)}, u32[]{:S(2)}, u32[]{:S(2)}) collective-permute-start(bf16[2,256,2,128]{3,1,2,0:T(8,128)(2,1)S(1)} %collective-permute-done.3), channel_id=1, source_target_pairs={{0,4},{4,8},{8,12},{12,16},{16,20},{20,24},{24,28},{28,32},{32,36}... | collective-permute-start | bytes 786440 | tf_op jit(solution)/shard_map/ppermute | solution.py:17
  85.8 12.5 %collective-permute-start.5 = (bf16[2,256,2,128]{3,1,2,0:T(8,128)(2,1)S(1)}, bf16[2,256,2,128]{3,1,2,0:T(8,128)(2,1)S(1)}, u32[]{:S(2)}, u32[]{:S(2)}) collective-permute-start(bf16[2,256,2,128]{3,1,2,0:T(8,128)(2,1)S(1)} %collective-permute-done.4), channel_id=1, source_target_pairs={{0,4},{4,8},{8,12},{12,16},{16,20},{20,24},{24,28},{28,32},{32,36}... | collective-permute-start | bytes 786440 | tf_op jit(solution)/shard_map/ppermute | solution.py:17
  98.3 12.5 %collective-permute-start.6 = (bf16[2,256,2,128]{3,1,2,0:T(8,128)(2,1)S(1)}, bf16[2,256,2,128]{3,1,2,0:T(8,128)(2,1)S(1)}, u32[]{:S(2)}, u32[]{:S(2)}) collective-permute-start(bf16[2,256,2,128]{3,1,2,0:T(8,128)(2,1)S(1)} %collective-permute-done.5), channel_id=1, source_target_pairs={{0,4},{4,8},{8,12},{12,16},{16,20},{20,24},{24,28},{28,32},{32,36}... | collective-permute-start | bytes 786440 | tf_op jit(solution)/shard_map/ppermute | solution.py:17
where the time goes:
time: 138 us
  waiting for transfers between devices  75.8 us (55%)
  matrix products  23.5 us (17%)
  starting transfers between devices  22.8 us (17%)
  other arithmetic  9.77 us (7%)
  local copies, waits for them, and re-layouts  5.64 us (4%)
    ppermute x7, waiting for transfers between devices, passed_along(): return lax.ppermute(shard, axis, pairs)  67.5 us
    dot_general x8, matrix products, update(): jnp.einsum('kgts,skd->kgtd', weights.astype(jnp.bfloat16), block[1], pref...  16.3 us
    ppermute x7, starting transfers between devices, passed_along(): return lax.ppermute(shard, axis, pairs)  15 us
    reduce_sum x8, other arithmetic, update(): total_new = total_old * fading + jnp.sum(weights, axis=-1)  8.16 us
    dot_general x8, matrix products, update(): jnp.einsum('tkgd,skd->kgts', grouped, block[0], preferred_element_type=jn...  7.25 us
    all_to_all x1, waiting for transfers between devices, body(): lax.all_to_all(values, 'kvh', split_axis=1, concat_axis=0, tiled=True)  5.8 us
    all_to_all x1, starting transfers between devices, body(): lax.all_to_all(keys, 'kvh', split_axis=1, concat_axis=0, tiled=True)  4.46 us
    all_to_all x1, starting transfers between devices, body(): lax.all_to_all(values, 'kvh', split_axis=1, concat_axis=0, tiled=True)  3.33 us
  transfers between devices with their start and end apart: 9, of which 9 were waited for; matrix products, arithmetic and copies ran while one was open for 7% of the time, Pallas kernels for 0%

commit v1 on v0

v1 whole, which is shorter than its diff:
```python
import math

import jax
import jax.numpy as jnp
from jax import lax
from jax.experimental import pallas as pl
from jax.experimental.pallas import tpu as pltpu
from jax.sharding import PartitionSpec as P

MESH = pl.DeviceIdType.MESH
NEG = -1e30
BIG = 1e30
EXP2_SCALE = math.log2(math.e) / math.sqrt(128)
NX, NYL, NZ = 4, 2, 8
BLK = 128
ONES = 16


def kernel(
    docs, q_hbm, k_hbm, v_hbm, out, q_in, kv_in, stage, cross, buf, qs, acc, top,
    in_sem, core_ssem, core_rsem, ssem, rsem,
):
    ctx = lax.axis_index("ctx")
    kvh = lax.axis_index("kvh")
    x = ctx % NX
    yl = (ctx // NX) % NYL
    z = ctx // (NX * NYL)
    yh = kvh // 2
    core = kvh % 2

    def device(x_, yl_, z_, yh_, core_):
        return (((z_ + NZ) % NZ) * (NX * NYL) + yl_ * NX + (x_ + NX) % NX, yh_ * 2 + core_)

    sibling = device(x, yl, z, yh, 1 - core)
    x_up = device(x + 1, yl, z, yh, core)
    x_down = device(x - 1, yl, z, yh, core)
    pair = device(x, 1 - yl, z, yh, core)
    other = device(x, 1 - yl, z, 1 - yh, core)
    z_up = device(x, yl, z + 1, yh, core)
    z_down = device(x, yl, z - 1, yh, core)

    barrier = pltpu.get_barrier_semaphore()
    for neighbour in (sibling, x_up, x_down, pair, other, z_up, z_down):
        pl.semaphore_signal(barrier, inc=1, device_id=neighbour, device_id_type=MESH)

    k_copy = pltpu.make_async_copy(k_hbm, kv_in.at[0], in_sem.at[0])
    v_copy = pltpu.make_async_copy(v_hbm, kv_in.at[1], in_sem.at[1])
    q_copy = pltpu.make_async_copy(q_hbm, q_in, in_sem.at[2])
    k_copy.start()
    v_copy.start()
    q_copy.start()

    for w, copy in enumerate((k_copy, v_copy)):
        copy.wait()
        heads = jnp.swapaxes(kv_in[w].astype(jnp.float32), 0, 1).astype(jnp.bfloat16)
        for g in range(4):
            for j in range(2):
                stage[g, j, w] = heads[2 * g + j]
    half = pl.ds(pl.multiple_of(core * 64, 64), 64)
    own_block, cross_block = yh, 1 - yh
    cross_group = (1 - yh) * 2 + core
    buf[0, own_block, :, :, half] = stage[kvh]
    cross[:, :, half] = stage[cross_group]

    pl.semaphore_wait(barrier, 7)

    swap_own = pltpu.make_async_remote_copy(
        src_ref=stage.at[yh * 2 + 1 - core],
        dst_ref=buf.at[0, own_block, :, :, half],
        send_sem=core_ssem.at[0],
        recv_sem=core_rsem.at[0],
        device_id=sibling,
        device_id_type=MESH,
    )
    swap_cross = pltpu.make_async_remote_copy(
        src_ref=stage.at[(1 - yh) * 2 + 1 - core],
        dst_ref=cross.at[:, :, half],
        send_sem=core_ssem.at[1],
        recv_sem=core_rsem.at[1],
        device_id=sibling,
        device_id_type=MESH,
    )
    swap_own.start()
    swap_cross.start()

    sent = []

    def push(src, slot, block, target, when=None):
        copy = pltpu.make_async_remote_copy(
            src_ref=src,
            dst_ref=buf.at[slot, block],
            send_sem=ssem.at[len(sent)],
            recv_sem=rsem.at[slot, block],
            device_id=target,
            device_id_type=MESH,
        )
        if when is None:
            copy.start()
        else:
            pl.when(when)(copy.start)
        sent.append((copy, when))

    def send(slot_from, slot_to, block, target, when=None):
        push(buf.at[slot_from, block], slot_to, block, target, when)

    def arrived(slot, block):
        pltpu.make_async_copy(
            buf.at[slot, block], buf.at[slot, block], rsem.at[slot, block]
        ).wait()

    step_up = jnp.where(x == 3, -3, 1)
    step_down = jnp.where(x == 0, 3, -1)
    relay_up = jnp.where(x == 3, 5, 1)
    relay_down = jnp.where(x == 0, 3, 7)
    crossed = jnp.where(yl == 1, 4, 9)

    swap_own.wait()
    send(0, 4, own_block, pair, yl == 0)
    send(0, 8, own_block, z_up)
    send(0, 1, own_block, x_up, x < 3)
    send(0, 3, own_block, x_down, x == 0)
    swap_cross.wait()
    push(cross, jnp.where(yl == 1, 9, 4), own_block, other)

    q_copy.wait()
    for j in range(2):
        for b in range(2):
            qs[j, pl.ds(b * 1024, 1024)] = q_in[
                b * BLK : (b + 1) * BLK, j * 8 : (j + 1) * 8, :
            ].reshape(1024, 128)

    arrived(crossed, cross_block)
    send(crossed, 0, cross_block, pair)
    send(9, 4, cross_block, z_up, yl == 0)
    send(4, 4 + step_up, cross_block, x_up, yl == 1)
    send(4, 4 + step_down, cross_block, x_down, yl == 1)
    arrived(8, own_block)
    send(8, 4, own_block, pair, yl == 1)
    send(8, 5, own_block, x_up, x == 3)
    send(8, 7, own_block, x_down, x > 0)
    arrived(0, cross_block)
    send(0, 8, cross_block, z_up)
    send(0, 1, cross_block, x_up, x < 3)
    send(0, 3, cross_block, x_down, x == 0)
    arrived(4, own_block)
    send(4, 4 + step_up, own_block, x_up)
    send(4, 4 + step_down, own_block, x_down)
    pl.when(yl == 0)(lambda: arrived(4, cross_block))
    send(4, 4 + step_up, cross_block, x_up, yl == 0)
    send(4, 4 + step_down, cross_block, x_down, yl == 0)
    arrived(8, cross_block)
    send(8, 5, cross_block, x_up, x == 3)
    send(8, 7, cross_block, x_down, x > 0)

    first = []
    for b in range(2):
        here = ctx * 2 + b
        end = jnp.int32(0)
        start = jnp.int32(0)
        for i in range(docs.shape[0]):
            end = end + docs[i]
            start = jnp.where(end <= here, end, start)
        first.append(start)

    def attend(slot, fresh):
        units = [(j, b) for j in range(2) for b in range(2)]
        kv = []
        for j in range(2):
            keys = jnp.concatenate([buf[slot, 0, j, 0], buf[slot, 1, j, 0]], axis=0)
            vals = jnp.concatenate([buf[slot, 0, j, 1], buf[slot, 1, j, 1]], axis=0)
            kv.append(
                (keys, jnp.concatenate([vals.T, jnp.ones((ONES, 2 * BLK), jnp.bfloat16)], axis=0))
            )

        def score(unit):
            j, b = unit
            return lax.dot_general(
                kv[j][0],
                qs[j, pl.ds(b * 1024, 1024), :],
                (((1,), (1,)), ((), ())),
                preferred_element_type=jnp.float32,
            )

        def soften(unit, scores):
            j, b = unit
            cols = pl.ds(b * 1024, 1024)
            parts = [scores[:BLK], scores[BLK:]]
            if fresh:
                keep = [ctx * 2 >= first[b], b == 1]
                row = lax.broadcasted_iota(jnp.int32, (BLK, 1024), 0)
                col = lax.broadcasted_iota(jnp.int32, (BLK, 1024), 1)
                parts[b] = jnp.where(row <= col // 8, parts[b], NEG)
            else:
                near = (ctx - slot) * 2
                keep = [near >= first[b], near + 1 >= first[b]]
            tops = [jnp.max(p, axis=0, keepdims=True) for p in parts]
            tops = [jnp.where(k, t, NEG) for k, t in zip(keep, tops)]
            new = jnp.maximum(tops[0], tops[1])
            fade = None
            if not fresh:
                old = top[j, :, cols]
                new = jnp.maximum(old, new)
                fade = jnp.exp2((old - new) * EXP2_SCALE)
            top[j, :, cols] = new
            weights = [
                jnp.exp2((p - jnp.where(k, new, BIG)) * EXP2_SCALE).astype(jnp.bfloat16)
                for k, p in zip(keep, parts)
            ]
            return jnp.concatenate(weights, axis=0), fade

        def add(unit, weights, fade):
            j, b = unit
            cols = pl.ds(b * 1024, 1024)
            product = lax.dot_general(
                kv[j][1], weights, (((1,), (0,)), ((), ())), preferred_element_type=jnp.float32
            )
            acc[j, :, cols] = product if fresh else acc[j, :, cols] * fade + product

        scores, waiting = score(units[0]), None
        for i, unit in enumerate(units):
            ahead = score(units[i + 1]) if i + 1 < len(units) else None
            if waiting is not None:
                add(*waiting)
            waiting = (unit, *soften(unit, scores))
            scores = ahead
        add(*waiting)

    attend(0, True)
    attend(4, False)
    for block in (own_block, cross_block):
        arrived(relay_up, block)
        send(relay_up, relay_up + step_up, block, x_up)
        arrived(relay_down, block)
        send(relay_down, relay_down + step_down, block, x_down)
    for slot in (1, 3, 5, 7, 2, 6):
        for block in (own_block, cross_block):
            pl.when(jnp.logical_and(relay_up != slot, relay_down != slot))(
                lambda: arrived(slot, block)
            )
        attend(slot, False)

    for j in range(2):
        for b in range(2):
            part = acc[j, :, pl.ds(b * 1024, 1024)]
            rows = (part[:BLK] / part[BLK : BLK + 1]).T
            out[b * BLK : (b + 1) * BLK, j * 8 : (j + 1) * 8, :] = rows.reshape(BLK, 8, 128).astype(
                jnp.bfloat16
            )
    for copy, when in sent:
        if when is None:
            copy.wait_send()
        else:
            pl.when(when)(copy.wait_send)


def body(queries, keys, values, doc_blocks):
    bf16, f32 = jnp.bfloat16, jnp.float32
    return pl.pallas_call(
        kernel,
        out_shape=jax.ShapeDtypeStruct(queries.shape, bf16),
        in_specs=[pl.BlockSpec(memory_space=pltpu.SMEM)] + [pl.BlockSpec(memory_space=pl.ANY)] * 3,
        out_specs=pl.BlockSpec(memory_space=pltpu.VMEM),
        scratch_shapes=[
            pltpu.VMEM(queries.shape, bf16),
            pltpu.VMEM((2,) + keys.shape, bf16),
            pltpu.VMEM((4, 2, 2, 64, 128), bf16),
            pltpu.VMEM((2, 2, BLK, 128), bf16),
            pltpu.VMEM((10, 2, 2, 2, BLK, 128), bf16),
            pltpu.VMEM((2, 2048, 128), bf16),
            pltpu.VMEM((2, BLK + ONES, 2048), f32),
            pltpu.VMEM((2, 1, 2048), f32),
            pltpu.SemaphoreType.DMA((3,)),
            pltpu.SemaphoreType.DMA((2,)),
            pltpu.SemaphoreType.DMA((2,)),
            pltpu.SemaphoreType.DMA((32,)),
            pltpu.SemaphoreType.DMA((10, 2)),
        ],
        compiler_params=pltpu.CompilerParams(
            collective_id=0, has_side_effects=True, vmem_limit_bytes=58 << 20
        ),
        name="gather_attend",
    )(doc_blocks, queries, keys, values)


def solution(mesh):
    in_specs = (
        P("ctx", "kvh", None),
        P(("ctx", "kvh"), None, None),
        P(("ctx", "kvh"), None, None),
        P(),
    )
    out_specs = P("ctx", "kvh", None)
    return jax.shard_map(body, mesh=mesh, in_specs=in_specs, out_specs=out_specs, check_vma=False)
```

time: 138 us -> 45.2 us (0.33)
  the two profiles are of different devices: /device:TPU:128 before, /device:TPU:2 now
where the time goes in v1:
time: 45.2 us; the launch traced here: 45.1 us
  Pallas kernels  42.7 us (94%)
  local copies, waits for them, and re-layouts  2.37 us (5%)
    pallas_call x1, Pallas kernels, body(): pl.pallas_call(kernel, out_shape=jax.ShapeDtypeStruct(queries.shape, bf16...  42.7 us
    unnamed x1, local copies, waits for them, and re-layouts  2.37 us

profile of v1, /device:TPU:2, one launch (start us, length us, event | category | flops | bytes accessed | tf_op | source)
XLA Modules:
  0.0 45.1 jit_solution(11230615418833608237)
XLA Ops:
  0.0 42.7 %gather_attend.1 = bf16[256,16,128]{2,1,0:T(8,128)(2,1)} custom-call(s32[32]{0:T(128)} %docs.1, bf16[256,16,128]{2,1,0:T(8,128)(2,1)} %q_hbm.1, bf16[64,8,128]{2,1,0:T(8,128)(2,1)} %k_hbm.1, bf16[64,8,128]{2,1,0:T(8,128)(2,1)} %v_hbm.1), custom_call_target="tpu_custom_call" | custom-call | tf_op jit(solution)/shard_map/gather_attend/pallas_call | solution.py:258
  42.7 2.4 %copy.6 = bf16[256,16,128]{2,1,0:T(8,128)(2,1)} copy(bf16[256,16,128]{2,1,0:T(8,128)(2,1)} %gather_attend.1) | data formatting | bytes 2097152

commit v2 on v1

--- a/solution.py
+++ b/solution.py
@@ -38,10 +38,24 @@
     other = device(x, 1 - yl, z, 1 - yh, core)
     z_up = device(x, yl, z + 1, yh, core)
     z_down = device(x, yl, z - 1, yh, core)
+    across = device(x, yl, z, 1 - yh, core)
+    diagonal = device(x, 1 - yl, z + 1, yh, core)
+    other_up = device(x, 1 - yl, z + 1, 1 - yh, core)
+    diagonal_back = device(x, 1 - yl, z - 1, yh, core)
+    other_back = device(x, 1 - yl, z - 1, 1 - yh, core)
 
     barrier = pltpu.get_barrier_semaphore()
-    for neighbour in (sibling, x_up, x_down, pair, other, z_up, z_down):
-        pl.semaphore_signal(barrier, inc=1, device_id=neighbour, device_id_type=MESH)
+    greeted = jnp.int32(0)
+    for neighbour, there in (
+        (sibling, True), (x_up, True), (x_down, True), (pair, True), (other, True), (across, True),
+        (z_up, z < NZ - 1), (diagonal, z < NZ - 1), (other_up, z < NZ - 1),
+        (z_down, z > 0), (diagonal_back, z > 0), (other_back, z > 0),
+    ):
+        there = jnp.logical_and(there, z >= 0)
+        pl.when(there)(
+            lambda: pl.semaphore_signal(barrier, inc=1, device_id=neighbour, device_id_type=MESH)
+        )
+        greeted = greeted + jnp.where(there, 1, 0)
 
     k_copy = pltpu.make_async_copy(k_hbm, kv_in.at[0], in_sem.at[0])
     v_copy = pltpu.make_async_copy(v_hbm, kv_in.at[1], in_sem.at[1])
@@ -62,7 +76,7 @@
     buf[0, own_block, :, :, half] = stage[kvh]
     cross[:, :, half] = stage[cross_group]
 
-    pl.semaphore_wait(barrier, 7)
+    pl.semaphore_wait(barrier, greeted)
 
     swap_own = pltpu.make_async_remote_copy(
         src_ref=stage.at[yh * 2 + 1 - core],
@@ -85,12 +99,12 @@
 
     sent = []
 
-    def push(src, slot, block, target, when=None):
+    def push(src, slot, block, j, target, when=None):
         copy = pltpu.make_async_remote_copy(
             src_ref=src,
-            dst_ref=buf.at[slot, block],
+            dst_ref=buf.at[slot, block, j],
             send_sem=ssem.at[len(sent)],
-            recv_sem=rsem.at[slot, block],
+            recv_sem=rsem.at[slot, block, j],
             device_id=target,
             device_id_type=MESH,
         )
@@ -100,27 +114,54 @@
             pl.when(when)(copy.start)
         sent.append((copy, when))
 
-    def send(slot_from, slot_to, block, target, when=None):
-        push(buf.at[slot_from, block], slot_to, block, target, when)
-
-    def arrived(slot, block):
-        pltpu.make_async_copy(
-            buf.at[slot, block], buf.at[slot, block], rsem.at[slot, block]
-        ).wait()
+    def send(slot_from, slot_to, block, j, target, when=None):
+        push(buf.at[slot_from, block, j], slot_to, block, j, target, when)
+
+    def arrived(slot, block, j, when=None):
+        ref = buf.at[slot, block, j]
+        copy = pltpu.make_async_copy(ref, ref, rsem.at[slot, block, j])
+        if when is None:
+            copy.wait()
+        else:
+            pl.when(when)(copy.wait)
+
+    has_near, has_far = ctx >= 4, z > 0
 
     step_up = jnp.where(x == 3, -3, 1)
     step_down = jnp.where(x == 0, 3, -1)
     relay_up = jnp.where(x == 3, 5, 1)
     relay_down = jnp.where(x == 0, 3, 7)
-    crossed = jnp.where(yl == 1, 4, 9)
 
     swap_own.wait()
-    send(0, 4, own_block, pair, yl == 0)
-    send(0, 8, own_block, z_up)
-    send(0, 1, own_block, x_up, x < 3)
-    send(0, 3, own_block, x_down, x == 0)
+    def wrap(value):
+        return (value + NX) % NX
+
+    def row_slot(at, source):
+        return jnp.where(source <= at, at - source, 8 + source - at)
+
+    def near_slot(at, source):
+        return 4 + at - source
+
+    below, above, opposite = wrap(x - 1), wrap(x + 1), wrap(x + 2)
+    for j in range(2):
+        send(0, row_slot(above, x), own_block, j, x_up)
+        send(0, row_slot(below, x), own_block, j, x_down)
     swap_cross.wait()
-    push(cross, jnp.where(yl == 1, 9, 4), own_block, other)
+    inside = z < NZ - 1
+    for j in range(2):
+        push(cross.at[j], 0, own_block, j, across)
+    for j in range(2):
+        target = tuple(jnp.where(yl == 0, p, d) for p, d in zip(pair, diagonal))
+        send(0, 4, own_block, j, target, jnp.logical_or(yl == 0, inside))
+    for j in range(2):
+        target = tuple(jnp.where(yl == 0, p, d) for p, d in zip(other, other_up))
+        push(cross.at[j], 4, own_block, j, target, jnp.logical_or(yl == 0, inside))
+
+    for slot in range(1, 8):
+
+        @pl.when(ctx < slot)
+        def _():
+            buf[slot] = jnp.zeros_like(buf[slot])
 
     q_copy.wait()
     for j in range(2):
@@ -129,28 +170,66 @@
                 b * BLK : (b + 1) * BLK, j * 8 : (j + 1) * 8, :
             ].reshape(1024, 128)
 
-    arrived(crossed, cross_block)
-    send(crossed, 0, cross_block, pair)
-    send(9, 4, cross_block, z_up, yl == 0)
-    send(4, 4 + step_up, cross_block, x_up, yl == 1)
-    send(4, 4 + step_down, cross_block, x_down, yl == 1)
-    arrived(8, own_block)
-    send(8, 4, own_block, pair, yl == 1)
-    send(8, 5, own_block, x_up, x == 3)
-    send(8, 7, own_block, x_down, x > 0)
-    arrived(0, cross_block)
-    send(0, 8, cross_block, z_up)
-    send(0, 1, cross_block, x_up, x < 3)
-    send(0, 3, cross_block, x_down, x == 0)
-    arrived(4, own_block)
-    send(4, 4 + step_up, own_block, x_up)
-    send(4, 4 + step_down, own_block, x_down)
-    pl.when(yl == 0)(lambda: arrived(4, cross_block))
-    send(4, 4 + step_up, cross_block, x_up, yl == 0)
-    send(4, 4 + step_down, cross_block, x_down, yl == 0)
-    arrived(8, cross_block)
-    send(8, 5, cross_block, x_up, x == 3)
-    send(8, 7, cross_block, x_down, x > 0)
+    def crossed(j):
+        arrived(0, cross_block, j)
+        send(0, 8, cross_block, j, z_up, z < NZ - 1)
+        send(0, 1, cross_block, j, x_up, x < 3)
+        send(0, 3, cross_block, j, x_down, x == 0)
+
+    def near(block, j):
+        arrived(4, block, j, has_near)
+        send(4, 4 + step_up, block, j, x_up, has_near)
+        send(4, 4 + step_down, block, j, x_down, has_near)
+
+    def far(block, j):
+        arrived(8, block, j, has_far)
+        send(8, 5, block, j, x_up, jnp.logical_and(has_far, x == 3))
+        send(8, 7, block, j, x_down, jnp.logical_and(has_far, x > 0))
+
+    def relay(block, j):
+        arrived(relay_up, block, j, ctx >= relay_up)
+        send(relay_up, relay_up + step_up, block, j, x_up, ctx >= relay_up)
+        arrived(relay_down, block, j, ctx >= relay_down)
+        send(relay_down, relay_down + step_down, block, j, x_down, ctx >= relay_down)
+
+    def across_row(slot_of, there=None):
+        arrived(slot_of(x, below), own_block, 0, there)
+        send(slot_of(x, below), slot_of(above, below), own_block, 0, x_up, there)
+        arrived(slot_of(x, above), own_block, 1, there)
+        send(slot_of(x, above), slot_of(below, above), own_block, 1, x_down, there)
+
+    def rest_of_row(slot_of, there=None):
+        arrived(slot_of(x, above), own_block, 0, there)
+        arrived(slot_of(x, below), own_block, 1, there)
+
+    def forward(source):
+        for j in range(2):
+            send(
+                row_slot(x, source), 8 + x - source, own_block, j, z_up,
+                jnp.logical_and(source > x, inside),
+            )
+
+    def forward_opposite():
+        for j in range(2):
+            arrived(row_slot(x, opposite), own_block, j)
+        forward(opposite)
+
+    def ready(slot):
+        if slot != 4:
+            there = ctx >= slot
+            for j in range(2):
+                passed_on = slot == near_slot(x, above if j else below)
+                open_own = jnp.logical_not(jnp.logical_or(slot <= x, passed_on))
+                arrived(slot, own_block, j, jnp.logical_and(there, open_own))
+                late = jnp.logical_and(relay_up != slot, relay_down != slot)
+                arrived(slot, cross_block, j, jnp.logical_and(there, late))
+
+    def both(step, *arguments):
+        def run():
+            for j in range(2):
+                step(*arguments, j)
+
+        return run
 
     first = []
     for b in range(2):
@@ -162,7 +241,8 @@
             start = jnp.where(end <= here, end, start)
         first.append(start)
 
-    def attend(slot, fresh):
+    def attend(slot, fresh, hooks=()):
+        hooks = list(hooks)
         units = [(j, b) for j in range(2) for b in range(2)]
         kv = []
         for j in range(2):
@@ -223,20 +303,28 @@
                 add(*waiting)
             waiting = (unit, *soften(unit, scores))
             scores = ahead
+            if i + 1 < len(units) and hooks:
+                hooks.pop(0)()
         add(*waiting)
-
-    attend(0, True)
-    attend(4, False)
-    for block in (own_block, cross_block):
-        arrived(relay_up, block)
-        send(relay_up, relay_up + step_up, block, x_up)
-        arrived(relay_down, block)
-        send(relay_down, relay_down + step_down, block, x_down)
+        for hook in hooks:
+            hook()
+
+    across_row(row_slot)
+    both(near, own_block)()
+    both(crossed)()
+    both(near, cross_block)()
+    rest_of_row(row_slot)
+    forward(above)
+    forward(below)
+
+    def settle():
+        across_row(near_slot, has_near)
+        forward_opposite()
+
+    attend(0, True, [both(far, cross_block), settle])
+    attend(4, False, [lambda: None, lambda: relay(cross_block, 0), lambda: relay(cross_block, 1)])
     for slot in (1, 3, 5, 7, 2, 6):
-        for block in (own_block, cross_block):
-            pl.when(jnp.logical_and(relay_up != slot, relay_down != slot))(
-                lambda: arrived(slot, block)
-            )
+        ready(slot)
         attend(slot, False)
 
     for j in range(2):
@@ -265,15 +353,15 @@
             pltpu.VMEM((2,) + keys.shape, bf16),
             pltpu.VMEM((4, 2, 2, 64, 128), bf16),
             pltpu.VMEM((2, 2, BLK, 128), bf16),
-            pltpu.VMEM((10, 2, 2, 2, BLK, 128), bf16),
+            pltpu.VMEM((12, 2, 2, 2, BLK, 128), bf16),
             pltpu.VMEM((2, 2048, 128), bf16),
             pltpu.VMEM((2, BLK + ONES, 2048), f32),
             pltpu.VMEM((2, 1, 2048), f32),
             pltpu.SemaphoreType.DMA((3,)),
             pltpu.SemaphoreType.DMA((2,)),
             pltpu.SemaphoreType.DMA((2,)),
-            pltpu.SemaphoreType.DMA((32,)),
-            pltpu.SemaphoreType.DMA((10, 2)),
+            pltpu.SemaphoreType.DMA((80,)),
+            pltpu.SemaphoreType.DMA((12, 2, 2)),
         ],
         compiler_params=pltpu.CompilerParams(
             collective_id=0, has_side_effects=True, vmem_limit_bytes=58 << 20

time: 45.2 us -> 40.2 us (0.89)
  the two profiles are of different devices: /device:TPU:2 before, /device:TPU:106 now
where the time goes in v2:
time: 40.2 us; the launch traced here: 40 us
  Pallas kernels  37.6 us (94%)
  local copies, waits for them, and re-layouts  2.37 us (6%)
    pallas_call x1, Pallas kernels, body(): pl.pallas_call(kernel, out_shape=jax.ShapeDtypeStruct(queries.shape, bf16...  37.6 us
    unnamed x1, local copies, waits for them, and re-layouts  2.37 us

profile of v2, /device:TPU:106, one launch (start us, length us, event | category | flops | bytes accessed | tf_op | source)
XLA Modules:
  0.0 40.0 jit_solution(13791390348932409244)
XLA Ops:
  0.0 37.6 %gather_attend.1 = bf16[256,16,128]{2,1,0:T(8,128)(2,1)} custom-call(s32[32]{0:T(128)} %docs.1, bf16[256,16,128]{2,1,0:T(8,128)(2,1)} %q_hbm.1, bf16[64,8,128]{2,1,0:T(8,128)(2,1)} %k_hbm.1, bf16[64,8,128]{2,1,0:T(8,128)(2,1)} %v_hbm.1), custom_call_target="tpu_custom_call" | custom-call | tf_op jit(solution)/shard_map/gather_attend/pallas_call | solution.py:346
  37.7 2.4 %copy.6 = bf16[256,16,128]{2,1,0:T(8,128)(2,1)} copy(bf16[256,16,128]{2,1,0:T(8,128)(2,1)} %gather_attend.1) | data formatting | bytes 2097152

commit v3 on v2

--- a/solution.py
+++ b/solution.py
@@ -18,7 +18,7 @@
 
 def kernel(
     docs, q_hbm, k_hbm, v_hbm, out, q_in, kv_in, stage, cross, buf, qs, acc, top,
-    in_sem, core_ssem, core_rsem, ssem, rsem,
+    in_sem, core_ssem, core_rsem, ssem, rsem, plane_sem,
 ):
     ctx = lax.axis_index("ctx")
     kvh = lax.axis_index("kvh")
@@ -45,17 +45,19 @@
     other_back = device(x, 1 - yl, z - 1, 1 - yh, core)
 
     barrier = pltpu.get_barrier_semaphore()
-    greeted = jnp.int32(0)
-    for neighbour, there in (
-        (sibling, True), (x_up, True), (x_down, True), (pair, True), (other, True), (across, True),
-        (z_up, z < NZ - 1), (diagonal, z < NZ - 1), (other_up, z < NZ - 1),
-        (z_down, z > 0), (diagonal_back, z > 0), (other_back, z > 0),
-    ):
-        there = jnp.logical_and(there, z >= 0)
-        pl.when(there)(
-            lambda: pl.semaphore_signal(barrier, inc=1, device_id=neighbour, device_id_type=MESH)
-        )
-        greeted = greeted + jnp.where(there, 1, 0)
+    def greet(device_id, semaphore, when=None):
+        def signal():
+            pl.semaphore_signal(semaphore, inc=1, device_id=device_id, device_id_type=MESH)
+
+        signal() if when is None else pl.when(when)(signal)
+
+    inside, behind = z < NZ - 1, z > 0
+    odd, even = yl == 1, yl == 0
+    for neighbour in (sibling, x_up, x_down, pair, other, across):
+        greet(neighbour, barrier)
+    greet(z_up, barrier, inside)
+    greet(diagonal, barrier, jnp.logical_and(inside, odd))
+    greet(other_up, barrier, jnp.logical_and(inside, odd))
 
     k_copy = pltpu.make_async_copy(k_hbm, kv_in.at[0], in_sem.at[0])
     v_copy = pltpu.make_async_copy(v_hbm, kv_in.at[1], in_sem.at[1])
@@ -76,7 +78,10 @@
     buf[0, own_block, :, :, half] = stage[kvh]
     cross[:, :, half] = stage[cross_group]
 
-    pl.semaphore_wait(barrier, greeted)
+    pl.semaphore_wait(barrier, 6 + jnp.where(behind, 1 + 2 * (1 - yl), 0))
+    greet(z_down, plane_sem, behind)
+    greet(diagonal_back, plane_sem, jnp.logical_and(behind, even))
+    greet(other_back, plane_sem, jnp.logical_and(behind, even))
 
     swap_own = pltpu.make_async_remote_copy(
         src_ref=stage.at[yh * 2 + 1 - core],
@@ -147,9 +152,9 @@
         send(0, row_slot(above, x), own_block, j, x_up)
         send(0, row_slot(below, x), own_block, j, x_down)
     swap_cross.wait()
-    inside = z < NZ - 1
     for j in range(2):
         push(cross.at[j], 0, own_block, j, across)
+    pl.when(jnp.logical_and(inside, odd))(lambda: pl.semaphore_wait(plane_sem, 3))
     for j in range(2):
         target = tuple(jnp.where(yl == 0, p, d) for p, d in zip(pair, diagonal))
         send(0, 4, own_block, j, target, jnp.logical_or(yl == 0, inside))
@@ -172,6 +177,8 @@
 
     def crossed(j):
         arrived(0, cross_block, j)
+        if j == 0:
+            pl.when(jnp.logical_and(inside, even))(lambda: pl.semaphore_wait(plane_sem, 1))
         send(0, 8, cross_block, j, z_up, z < NZ - 1)
         send(0, 1, cross_block, j, x_up, x < 3)
         send(0, 3, cross_block, j, x_down, x == 0)
@@ -241,21 +248,23 @@
             start = jnp.where(end <= here, end, start)
         first.append(start)
 
-    def attend(slot, fresh, hooks=()):
+    def attend(slot, hooks=()):
         hooks = list(hooks)
+        fresh = slot == 0
         units = [(j, b) for j in range(2) for b in range(2)]
-        kv = []
-        for j in range(2):
-            keys = jnp.concatenate([buf[slot, 0, j, 0], buf[slot, 1, j, 0]], axis=0)
-            vals = jnp.concatenate([buf[slot, 0, j, 1], buf[slot, 1, j, 1]], axis=0)
-            kv.append(
-                (keys, jnp.concatenate([vals.T, jnp.ones((ONES, 2 * BLK), jnp.bfloat16)], axis=0))
-            )
+        if slot == 7:
+            units = [(j, 0) for j in range(2)]
+
+        def blocks(b):
+            if slot == 7:
+                return (1,)
+            return (0,) if fresh and b == 0 else (0, 1)
 
         def score(unit):
             j, b = unit
+            keys = [buf[slot, e, j, 0] for e in blocks(b)]
             return lax.dot_general(
-                kv[j][0],
+                jnp.concatenate(keys, axis=0),
                 qs[j, pl.ds(b * 1024, 1024), :],
                 (((1,), (1,)), ((), ())),
                 preferred_element_type=jnp.float32,
@@ -264,18 +273,17 @@
         def soften(unit, scores):
             j, b = unit
             cols = pl.ds(b * 1024, 1024)
-            parts = [scores[:BLK], scores[BLK:]]
-            if fresh:
-                keep = [ctx * 2 >= first[b], b == 1]
-                row = lax.broadcasted_iota(jnp.int32, (BLK, 1024), 0)
-                col = lax.broadcasted_iota(jnp.int32, (BLK, 1024), 1)
-                parts[b] = jnp.where(row <= col // 8, parts[b], NEG)
-            else:
-                near = (ctx - slot) * 2
-                keep = [near >= first[b], near + 1 >= first[b]]
-            tops = [jnp.max(p, axis=0, keepdims=True) for p in parts]
-            tops = [jnp.where(k, t, NEG) for k, t in zip(keep, tops)]
-            new = jnp.maximum(tops[0], tops[1])
+            parts, keep, tops = [], [], []
+            for i, e in enumerate(blocks(b)):
+                part = scores[i * BLK : (i + 1) * BLK]
+                if fresh and e == b:
+                    row = lax.broadcasted_iota(jnp.int32, (BLK, 1024), 0)
+                    col = lax.broadcasted_iota(jnp.int32, (BLK, 1024), 1)
+                    part = jnp.where(row <= col // 8, part, NEG)
+                parts.append(part)
+                keep.append((ctx - slot) * 2 + e >= first[b])
+                tops.append(jnp.where(keep[-1], jnp.max(part, axis=0, keepdims=True), NEG))
+            new = tops[0] if len(tops) == 1 else jnp.maximum(tops[0], tops[1])
             fade = None
             if not fresh:
                 old = top[j, :, cols]
@@ -291,8 +299,12 @@
         def add(unit, weights, fade):
             j, b = unit
             cols = pl.ds(b * 1024, 1024)
+            vals = jnp.concatenate([buf[slot, e, j, 1] for e in blocks(b)], axis=0)
+            ones = jnp.ones((ONES, vals.shape[0]), jnp.bfloat16)
             product = lax.dot_general(
-                kv[j][1], weights, (((1,), (0,)), ((), ())), preferred_element_type=jnp.float32
+                jnp.concatenate([vals.T, ones], axis=0), weights,
+                (((1,), (0,)), ((), ())),
+                preferred_element_type=jnp.float32,
             )
             acc[j, :, cols] = product if fresh else acc[j, :, cols] * fade + product
 
@@ -321,11 +333,11 @@
         across_row(near_slot, has_near)
         forward_opposite()
 
-    attend(0, True, [both(far, cross_block), settle])
-    attend(4, False, [lambda: None, lambda: relay(cross_block, 0), lambda: relay(cross_block, 1)])
+    attend(0, [both(far, cross_block), settle])
+    attend(4, [lambda: None, lambda: relay(cross_block, 0), lambda: relay(cross_block, 1)])
     for slot in (1, 3, 5, 7, 2, 6):
         ready(slot)
-        attend(slot, False)
+        attend(slot)
 
     for j in range(2):
         for b in range(2):
@@ -362,6 +374,7 @@
             pltpu.SemaphoreType.DMA((2,)),
             pltpu.SemaphoreType.DMA((80,)),
             pltpu.SemaphoreType.DMA((12, 2, 2)),
+            pltpu.SemaphoreType.REGULAR,
         ],
         compiler_params=pltpu.CompilerParams(
             collective_id=0, has_side_effects=True, vmem_limit_bytes=58 << 20

time: 40.2 us -> 36.7 us (0.913)
  the two profiles are of different devices: /device:TPU:106 before, /device:TPU:130 now
where the time goes in v3:
time: 36.7 us; the launch traced here: 36.6 us
  Pallas kernels  34.2 us (93%)
  local copies, waits for them, and re-layouts  2.37 us (6%)
    pallas_call x1, Pallas kernels, body(): pl.pallas_call(kernel, out_shape=jax.ShapeDtypeStruct(queries.shape, bf16...  34.2 us
    unnamed x1, local copies, waits for them, and re-layouts  2.37 us

profile of v3, /device:TPU:130, one launch (start us, length us, event | category | flops | bytes accessed | tf_op | source)
XLA Modules:
  0.0 36.6 jit_solution(16424428985886094690)
XLA Ops:
  0.0 34.2 %gather_attend.1 = bf16[256,16,128]{2,1,0:T(8,128)(2,1)} custom-call(s32[32]{0:T(128)} %docs.1, bf16[256,16,128]{2,1,0:T(8,128)(2,1)} %q_hbm.1, bf16[64,8,128]{2,1,0:T(8,128)(2,1)} %k_hbm.1, bf16[64,8,128]{2,1,0:T(8,128)(2,1)} %v_hbm.1), custom_call_target="tpu_custom_call" | custom-call | tf_op jit(solution)/shard_map/gather_attend/pallas_call | solution.py:358
  34.2 2.4 %copy.6 = bf16[256,16,128]{2,1,0:T(8,128)(2,1)} copy(bf16[256,16,128]{2,1,0:T(8,128)(2,1)} %gather_attend.1) | data formatting | bytes 2097152

commit v4 on v3

--- a/solution.py
+++ b/solution.py
@@ -17,8 +17,8 @@
 
 
 def kernel(
-    docs, q_hbm, k_hbm, v_hbm, out, q_in, kv_in, stage, cross, buf, qs, acc, top,
-    in_sem, core_ssem, core_rsem, ssem, rsem, plane_sem,
+    docs, q_hbm, k_hbm, v_hbm, out, q_in, kv_in, stage, buf, qs, acc, top,
+    in_sem, ssem, rsem, plane_sem,
 ):
     ctx = lax.axis_index("ctx")
     kvh = lax.axis_index("kvh")
@@ -53,11 +53,17 @@
 
     inside, behind = z < NZ - 1, z > 0
     odd, even = yl == 1, yl == 0
-    for neighbour in (sibling, x_up, x_down, pair, other, across):
-        greet(neighbour, barrier)
+    def cores(neighbour):
+        return neighbour, (neighbour[0], neighbour[1] + 1 - 2 * core)
+
+    greet(sibling, barrier)
+    for neighbour in (x_up, x_down, pair, other, across):
+        for device_id in cores(neighbour):
+            greet(device_id, barrier)
     greet(z_up, barrier, inside)
-    greet(diagonal, barrier, jnp.logical_and(inside, odd))
-    greet(other_up, barrier, jnp.logical_and(inside, odd))
+    for neighbour in (diagonal, other_up):
+        for device_id in cores(neighbour):
+            greet(device_id, barrier, jnp.logical_and(inside, odd))
 
     k_copy = pltpu.make_async_copy(k_hbm, kv_in.at[0], in_sem.at[0])
     v_copy = pltpu.make_async_copy(v_hbm, kv_in.at[1], in_sem.at[1])
@@ -74,40 +80,20 @@
                 stage[g, j, w] = heads[2 * g + j]
     half = pl.ds(pl.multiple_of(core * 64, 64), 64)
     own_block, cross_block = yh, 1 - yh
-    cross_group = (1 - yh) * 2 + core
     buf[0, own_block, :, :, half] = stage[kvh]
-    cross[:, :, half] = stage[cross_group]
-
-    pl.semaphore_wait(barrier, 6 + jnp.where(behind, 1 + 2 * (1 - yl), 0))
+
+    pl.semaphore_wait(barrier, 11 + jnp.where(behind, 1 + 4 * (1 - yl), 0))
     greet(z_down, plane_sem, behind)
-    greet(diagonal_back, plane_sem, jnp.logical_and(behind, even))
-    greet(other_back, plane_sem, jnp.logical_and(behind, even))
-
-    swap_own = pltpu.make_async_remote_copy(
-        src_ref=stage.at[yh * 2 + 1 - core],
-        dst_ref=buf.at[0, own_block, :, :, half],
-        send_sem=core_ssem.at[0],
-        recv_sem=core_rsem.at[0],
-        device_id=sibling,
-        device_id_type=MESH,
-    )
-    swap_cross = pltpu.make_async_remote_copy(
-        src_ref=stage.at[(1 - yh) * 2 + 1 - core],
-        dst_ref=cross.at[:, :, half],
-        send_sem=core_ssem.at[1],
-        recv_sem=core_rsem.at[1],
-        device_id=sibling,
-        device_id_type=MESH,
-    )
-    swap_own.start()
-    swap_cross.start()
+    for neighbour in (diagonal_back, other_back):
+        for device_id in cores(neighbour):
+            greet(device_id, plane_sem, jnp.logical_and(behind, even))
 
     sent = []
 
-    def push(src, slot, block, j, target, when=None):
+    def push(src, dst, slot, block, j, target, when=None):
         copy = pltpu.make_async_remote_copy(
             src_ref=src,
-            dst_ref=buf.at[slot, block, j],
+            dst_ref=dst,
             send_sem=ssem.at[len(sent)],
             recv_sem=rsem.at[slot, block, j],
             device_id=target,
@@ -120,7 +106,16 @@
         sent.append((copy, when))
 
     def send(slot_from, slot_to, block, j, target, when=None):
-        push(buf.at[slot_from, block, j], slot_to, block, j, target, when)
+        push(
+            buf.at[slot_from, block, j], buf.at[slot_to, block, j], slot_to, block, j, target, when
+        )
+
+    def send_half(slot, j, side, target, when=None):
+        for c in (core, 1 - core):
+            push(
+                stage.at[side * 2 + c, j], buf.at[slot, own_block, j, :, half],
+                slot, own_block, j, (target[0], (target[1] // 2) * 2 + c), when,
+            )
 
     def arrived(slot, block, j, when=None):
         ref = buf.at[slot, block, j]
@@ -137,7 +132,12 @@
     relay_up = jnp.where(x == 3, 5, 1)
     relay_down = jnp.where(x == 0, 3, 7)
 
-    swap_own.wait()
+    for j in range(2):
+        push(
+            stage.at[yh * 2 + 1 - core, j], buf.at[0, own_block, j, :, half],
+            0, own_block, j, sibling,
+        )
+
     def wrap(value):
         return (value + NX) % NX
 
@@ -149,18 +149,17 @@
 
     below, above, opposite = wrap(x - 1), wrap(x + 1), wrap(x + 2)
     for j in range(2):
-        send(0, row_slot(above, x), own_block, j, x_up)
-        send(0, row_slot(below, x), own_block, j, x_down)
-    swap_cross.wait()
-    for j in range(2):
-        push(cross.at[j], 0, own_block, j, across)
-    pl.when(jnp.logical_and(inside, odd))(lambda: pl.semaphore_wait(plane_sem, 3))
+        send_half(row_slot(above, x), j, yh, x_up)
+        send_half(row_slot(below, x), j, yh, x_down)
+    for j in range(2):
+        send_half(0, j, 1 - yh, across)
+    pl.when(jnp.logical_and(inside, odd))(lambda: pl.semaphore_wait(plane_sem, 5))
     for j in range(2):
         target = tuple(jnp.where(yl == 0, p, d) for p, d in zip(pair, diagonal))
-        send(0, 4, own_block, j, target, jnp.logical_or(yl == 0, inside))
+        send_half(4, j, yh, target, jnp.logical_or(yl == 0, inside))
     for j in range(2):
         target = tuple(jnp.where(yl == 0, p, d) for p, d in zip(other, other_up))
-        push(cross.at[j], 4, own_block, j, target, jnp.logical_or(yl == 0, inside))
+        send_half(4, j, 1 - yh, target, jnp.logical_or(yl == 0, inside))
 
     for slot in range(1, 8):
 
@@ -333,6 +332,9 @@
         across_row(near_slot, has_near)
         forward_opposite()
 
+    for j in range(2):
+        ref = buf.at[0, own_block, j, :, half]
+        pltpu.make_async_copy(ref, ref, rsem.at[0, own_block, j]).wait()
     attend(0, [both(far, cross_block), settle])
     attend(4, [lambda: None, lambda: relay(cross_block, 0), lambda: relay(cross_block, 1)])
     for slot in (1, 3, 5, 7, 2, 6):
@@ -364,14 +366,11 @@
             pltpu.VMEM(queries.shape, bf16),
             pltpu.VMEM((2,) + keys.shape, bf16),
             pltpu.VMEM((4, 2, 2, 64, 128), bf16),
-            pltpu.VMEM((2, 2, BLK, 128), bf16),
             pltpu.VMEM((12, 2, 2, 2, BLK, 128), bf16),
             pltpu.VMEM((2, 2048, 128), bf16),
             pltpu.VMEM((2, BLK + ONES, 2048), f32),
             pltpu.VMEM((2, 1, 2048), f32),
             pltpu.SemaphoreType.DMA((3,)),
-            pltpu.SemaphoreType.DMA((2,)),
-            pltpu.SemaphoreType.DMA((2,)),
             pltpu.SemaphoreType.DMA((80,)),
             pltpu.SemaphoreType.DMA((12, 2, 2)),
             pltpu.SemaphoreType.REGULAR,

time: 36.7 us -> 36.5 us (level)
  the two profiles are of different devices: /device:TPU:130 before, /device:TPU:128 now
where the time goes in v4:
time: 36.5 us; the launch traced here: 36.1 us
  Pallas kernels  33.7 us (92%)
  local copies, waits for them, and re-layouts  2.37 us (6%)
    pallas_call x1, Pallas kernels, body(): pl.pallas_call(kernel, out_shape=jax.ShapeDtypeStruct(queries.shape, bf16...  33.7 us
    unnamed x1, local copies, waits for them, and re-layouts  2.37 us

profile of v4, /device:TPU:128, one launch (start us, length us, event | category | flops | bytes accessed | tf_op | source)
XLA Modules:
  0.0 36.1 jit_solution(17052647891049746537)
XLA Ops:
  0.0 33.7 %gather_attend.1 = bf16[256,16,128]{2,1,0:T(8,128)(2,1)} custom-call(s32[32]{0:T(128)} %docs.1, bf16[256,16,128]{2,1,0:T(8,128)(2,1)} %q_hbm.1, bf16[64,8,128]{2,1,0:T(8,128)(2,1)} %k_hbm.1, bf16[64,8,128]{2,1,0:T(8,128)(2,1)} %v_hbm.1), custom_call_target="tpu_custom_call" | custom-call | tf_op jit(solution)/shard_map/gather_attend/pallas_call | solution.py:360
  33.7 2.4 %copy.6 = bf16[256,16,128]{2,1,0:T(8,128)(2,1)} copy(bf16[256,16,128]{2,1,0:T(8,128)(2,1)} %gather_attend.1) | data formatting | bytes 2097152
